TPU v7x, 32 devices: a whole 2x2x4 slice. The times are simulated.
32 devices in a mesh: ctx: 8 (over z, y), head: 4 (over x, core).
Axes of the slice: x: 2, y: 2, z: 4, core: 2. Of those that a mesh axis runs over, the one named last changes fastest.
Arguments:
- query: bfloat16 [8, 64, 576], P('ctx', 'head'), may hold values from -20 to 20
- cache: bfloat16 [32768, 576], P('ctx'), may hold values from -20 to 20
- cotangent: bfloat16 [8, 64, 512], P('ctx', 'head'), may hold values from -6 to 6
- positions: int32 [8], P('ctx'), may hold values from 0 to 262143
- visible: int32 [8], replicated, may hold values from 128 to 32768, as said below
Outputs:
- attention: bfloat16 [8, 64, 512], P('ctx', 'head')
- grad_query: float32 [8, 64, 576], P('ctx', 'head')
- grad_cache: bfloat16 [32768, 576], P('ctx')
Inputs may be any that keep to these rules, and one draw needn't show every extreme that they name: `visible`: each entry is a multiple of 128; some rollout token sees all 32768 prompt tokens.
All inputs are finite; a program needn't handle non-finite values.
Results may differ from a plain program's by a relative error of at most 0.01855.
Values may be sent and summed in bfloat16 or wider, within the bound.
No kernel may reach another device: no remote copies, remote signals or barrier semaphores. Data moves between devices by JAX's collectives and lax.ppermute only.
A program may use at most 128 MiB of HBM per device.

v0:
```python
import jax
import jax.numpy as jnp
import numpy as np
from jax import lax
from jax.sharding import PartitionSpec as P

softmax_scale = 192.0 ** (-0.5)
position_bits = 18
masked_value = -1e30


def rotation(positions, half_width):
    frequency = 10000.0 ** (-np.arange(half_width) / half_width)
    angles = np.outer(2.0 ** np.arange(position_bits), frequency)
    cosine_table = jnp.asarray(np.cos(angles), jnp.float32)
    sine_table = jnp.asarray(np.sin(angles), jnp.float32)
    cosines = jnp.ones((positions.shape[0], half_width), jnp.float32)
    sine_part = jnp.zeros((positions.shape[0], half_width), jnp.float32)
    for bit_index in range(position_bits):
        switch = (positions // 2**bit_index % 2).astype(jnp.float32)[:, None]
        step_cos = 1.0 + switch * (cosine_table[bit_index] - 1.0)
        step_sin = switch * sine_table[bit_index]
        cosines, sine_part = (
            cosines * step_cos - sine_part * step_sin,
            sine_part * step_cos + cosines * step_sin,
        )
    return (cosines[:, None, :], sine_part[:, None, :])


def rotate(tensor, cosines, sine_part, value_width, inverse):
    half_width = cosines.shape[-1]
    lower = tensor[..., value_width : value_width + half_width]
    upper = tensor[..., value_width + half_width :]
    if inverse:
        sine_part = -sine_part
    new_lower = lower * cosines - upper * sine_part
    new_upper = lower * sine_part + upper * cosines
    return jnp.concatenate([tensor[..., :value_width], new_lower, new_upper], axis=-1)


def body(query, cache, cotangent, positions, visible):
    value_width = cotangent.shape[-1]
    half_width = (query.shape[-1] - value_width) // 2
    extra_width = cache.shape[1] - value_width
    cosines, sine_part = rotation(positions, half_width)
    rotated = rotate(query.astype(jnp.float32), cosines, sine_part, value_width, False).astype(
        jnp.bfloat16
    )
    rotated, gradients = (
        lax.all_gather(rotated, "ctx", axis=0, tiled=True),
        lax.all_gather(cotangent, "ctx", axis=0, tiled=True),
    )
    block_rows = cache.shape[0]
    first_key = lax.axis_index("ctx") * block_rows
    key_index = first_key + jnp.arange(block_rows)
    allowed = key_index[None, None, :] < visible[:, None, None]
    scores = (
        jnp.einsum("thl,kl->thk", rotated, cache, preferred_element_type=jnp.float32)
        * softmax_scale
    )
    scores = jnp.where(allowed, scores, masked_value)
    local_peak = jnp.max(scores, axis=2)
    peak = lax.pmax(local_peak, "ctx")
    weights = jnp.where(allowed, jnp.exp(scores - peak[..., None]), 0.0)
    local_mass = jnp.sum(weights, axis=2)
    mass = lax.psum(local_mass, "ctx")
    probs = weights / mass[..., None]
    prob_low = probs.astype(jnp.bfloat16)
    values = cache[:, :value_width]
    attended = jnp.einsum("thk,kv->thv", prob_low, values, preferred_element_type=jnp.float32)
    attention = lax.psum_scatter(attended, "ctx", scatter_dimension=0, tiled=True).astype(
        jnp.bfloat16
    )
    grad_probs = jnp.einsum("thv,kv->thk", gradients, values, preferred_element_type=jnp.float32)
    local_delta = jnp.sum(prob_low.astype(jnp.float32) * grad_probs, axis=2)
    delta = lax.psum(local_delta, "ctx")
    grad_scores = (probs * (grad_probs - delta[..., None]) * softmax_scale).astype(jnp.bfloat16)
    grad_rotated = jnp.einsum("thk,kl->thl", grad_scores, cache, preferred_element_type=jnp.float32)
    grad_latent = jnp.einsum(
        "thk,thl->kl", grad_scores, rotated, preferred_element_type=jnp.float32
    )
    grad_value = jnp.einsum("thk,thv->kv", prob_low, gradients, preferred_element_type=jnp.float32)
    grad_latent = grad_latent + jnp.pad(grad_value, ((0, 0), (0, extra_width)))
    grad_cache = lax.psum(grad_latent, "head").astype(jnp.bfloat16)
    grad_rotated = lax.psum_scatter(grad_rotated, "ctx", scatter_dimension=0, tiled=True)
    grad_query = rotate(grad_rotated, cosines, sine_part, value_width, True)
    return (attention, grad_query, grad_cache)


def solution(mesh):
    placed = (P("ctx", "head", None), P("ctx", None), P("ctx", "head", None), P("ctx"), P())
    return jax.shard_map(
        body,
        mesh=mesh,
        in_specs=placed,
        out_specs=(P("ctx", "head", None), P("ctx", "head", None), P("ctx", None)),
        check_vma=False,
    )
```

profile of v0, /device:TPU:0, one launch (start us, length us, event | category | flops | bytes accessed | tf_op | source)
XLA Modules:
  0.0 339.2 jit_solution(13869444425280142998)
XLA Ops:
  7.2 0.0 reduce-scatter.3.cloned.1.call-start
  8.3 0.7 slice.130
  9.0 0.7 convert_element_type.83
  9.8 32.5 %all_gather.7 = bf16[8,16,512]{2,1,0:T(8,128)(2,1)S(1)} all-gather(bf16[1,16,512]{2,1,0:T(8,128)(2,1)} %param.9), channel_id=1, replica_groups=mesh['ctx'=8,'head'=4] {'ctx'}, dimensions={0}, use_global_device_ids=true | all-gather | bytes 147456 | tf_op jit(solution)/shard_map/all_gather | solution.py:51
  42.3 0.7 fusion.15
  43.0 0.7 fusion.18
  43.7 0.7 fusion.22
  44.5 0.7 fusion.26
  45.2 0.7 fusion.30
  46.0 0.7 fusion.34
  46.7 0.7 fusion.38
  47.5 0.7 fusion.42
  48.2 0.7 fusion.50
  49.0 0.7 fusion.49
  49.7 0.1 subtract_convert_fusion
  49.7 0.1 pad_maximum_fusion.1
  49.8 30.6 %all_gather.6 = bf16[8,16,576]{2,1,0:T(8,128)(2,1)S(1)} all-gather(bf16[1,16,576]{2,1,0:T(8,128)(2,1)S(1)} %pad_maximum_fusion.1), channel_id=1, replica_groups=mesh['ctx'=8,'head'=4] {'ctx'}, dimensions={0}, use_global_device_ids=true | all-gather | bytes 165888 | tf_op jit(solution)/shard_map/all_gather | solution.py:50
  80.4 0.7 broadcast_compare_fusion
  81.1 3.6 %fusion.69 = (f32[8,16]{1,0:T(8,128)S(1)}, f32[8,16,4096]{2,1,0:T(8,128)S(1)}) fusion(bf16[8,16,576]{2,1,0:T(8,128)(2,1)S(1)} %all_gather.6, bf16[4096,576]{0,1:T(8,128)(2,1)} %param.8, pred[8,4096]{1,0:T(8,128)(4,1)S(1)} %broadcast_compare_fusion), kind=kOutput, calls=%fused_computation.119 | convolution fusion | flops 605552512 | bytes 6996480 | tf_op jit(solution)/shard_map/thl,kl->thk/dot_general | solution.py:58
  84.8 21.4 %pmax.7 = f32[8,16]{1,0:T(8,128)S(1)} all-reduce(f32[8,16]{1,0:T(8,128)S(1)} %get-tuple-element.36), channel_id=1, replica_groups=mesh['ctx'=8,'head'=4] {'ctx'}, use_global_device_ids=true, to_apply=%region_1.2 | all-reduce | flops 128 | bytes 1024 | tf_op jit(solution)/shard_map/pmax | solution.py:63
  106.1 0.0 slice-start
  106.1 0.6 fusion.11
  106.7 17.1 %psum.21 = f32[8,16]{1,0:T(8,128)S(1)} all-reduce(f32[8,16]{1,0:T(8,128)S(1)} %fusion.11), channel_id=1, replica_groups=mesh['ctx'=8,'head'=4] {'ctx'}, use_global_device_ids=true, to_apply=%region_3.4 | all-reduce | flops 128 | bytes 1024 | tf_op jit(solution)/shard_map/psum | solution.py:66
  123.8 0.0 slice-start.1
  123.8 4.9 %multiply_reduce_fusion = (f32[8,16]{1,0:T(8,128)S(1)}, bf16[8,16,4096]{2,1,0:T(8,128)(2,1)S(1)}, f32[8,16,4096]{2,1,0:T(8,128)}) fusion(f32[8,16]{1,0:T(8,128)S(1)} %psum.21, f32[8,16,4096]{2,1,0:T(8,128)S(1)} %get-tuple-element.37, f32[8,16]{1,0:T(8,128)S(1)} %pmax.7, pred[8,4096]{1,0:T(8,128)(4,1)S(1)} %broadcast_compare_fusion, ...), kind=kOutput, calls=%fused_computation.14 | convolution fusion | flops 540540800 | bytes 9602560 | tf_op jit(solution)/shard_map/thv,kv->thk/dot_general | solution.py:74
  128.7 0.0 copy-start
  128.7 1.0 copy-done
  129.7 0.0 slice-done
  129.7 0.0 slice-done.1
  129.7 2.3 fusion.6
  132.0 0.0 reduce-scatter.3.cloned.1.call-update
  132.0 0.0 reduce-scatter.5.cloned.1.call-start
  132.1 19.1 %psum.22 = f32[8,16]{1,0:T(8,128)S(1)} all-reduce(f32[8,16]{1,0:T(8,128)S(1)} %get-tuple-element.7), channel_id=1, replica_groups=mesh['ctx'=8,'head'=4] {'ctx'}, use_global_device_ids=true, to_apply=%region_6.7 | all-reduce | flops 128 | bytes 1024 | tf_op jit(solution)/shard_map/psum | solution.py:76
  151.2 2.3 multiply_convert_fusion
  153.6 0.0 copy-start.1
  153.6 4.9 %fusion.1 = f32[8,16,576]{2,1,0:T(8,128)} fusion(bf16[8,16,4096]{2,1,0:T(8,128)(2,1)S(1)} %multiply_convert_fusion, bf16[4096,576]{0,1:T(8,128)(2,1)} %param.8), kind=kOutput, calls=%fused_computation.4 | convolution fusion | flops 603979776 | bytes 6062080 | tf_op jit(solution)/shard_map/thk,kl->thl/dot_general | solution.py:78
  158.5 0.0 reduce-scatter.5.cloned.1.call-update
  158.5 0.0 copy-done.1
  158.5 1.3 convolution_bitcast_fusion
  159.8 5.1 %bitcast_add_fusion = f32[4096,576]{0,1:T(8,128)} fusion(f32[4096,512]{0,1:T(8,128)S(1)} %convolution_bitcast_fusion, bf16[8,16,4096]{2,1,0:T(8,128)(2,1)S(1)} %multiply_convert_fusion, bf16[8,16,576]{2,1,0:T(8,128)(2,1)S(1)} %all_gather.6), kind=kOutput, calls=%fused_computation | convolution fusion | flops 606339072 | bytes 19021824 | tf_op jit(solution)/shard_map/thk,thl->kl/dot_general | solution.py:79
  164.9 163.8 %all-reduce.2 = bf16[4096,576]{0,1:T(8,128)(2,1)} all-reduce(f32[4096,576]{0,1:T(8,128)} %bitcast_add_fusion), channel_id=1, replica_groups=mesh['ctx'=8,'head'=4] {'head'}, use_global_device_ids=true, to_apply=%region_8.9 | all-reduce | flops 2359296 | bytes 14155776 | tf_op jit(solution)/shard_map/psum | solution.py:84
  328.7 0.0 reduce-scatter.3.cloned.1.call-done
  328.7 1.4 convert_element_type.103
  330.0 0.0 reduce-scatter.5.cloned.1.call-done
  330.0 0.8 slice.175
  330.8 0.9 multiply_subtract_fusion
  331.7 0.7 pad_maximum_fusion
  (2 shorter events, 0.0 us)
Async XLA Ops:
  7.2 321.5 %reduce-scatter.3.cloned.1.call-start = ((), (), s32[]{:S(2)}) async-start(), calls=%async_computation.2 | async-start | bytes 294912 | tf_op jit(solution)/shard_map/reduce_scatter | solution.py:71
  106.1 23.6 %slice-start = ((s8[4718592]{0:T(1024)(128)(4,1)}), s8[524288]{0:T(1024)(128)(4,1)S(1)}, s32[]{:S(2)}) async-start(s8[4718592]{0:T(1024)(128)(4,1)} %bitcast.51), calls=%async_computation.4 | async-start | bytes 1048576
  123.8 5.9 %slice-start.1 = ((s8[4718592]{0:T(1024)(128)(4,1)}), s8[4194304]{0:T(1024)(128)(4,1)S(1)}, s32[]{:S(2)}) async-start(s8[4718592]{0:T(1024)(128)(4,1)} %bitcast.51), calls=%async_computation.5 | async-start | bytes 8388608
  128.7 1.0 copy-start
  132.0 198.0 %reduce-scatter.5.cloned.1.call-start = ((), (), s32[]{:S(2)}) async-start(), calls=%async_computation.3 | async-start | bytes 368640 | tf_op jit(solution)/shard_map/reduce_scatter | solution.py:85
  153.6 4.9 %copy-start.1 = (bf16[8,16,4096]{2,1,0:T(8,128)(2,1)S(1)}, bf16[8,16,4096]{2,1,0:T(8,128)(2,1)}, u32[]{:S(2)}) copy-start(bf16[8,16,4096]{2,1,0:T(8,128)(2,1)} %copy-done) | copy-start | bytes 3145732
Sparse Core Ops, SparseCore 0:
  132.1 60.7 reduce-scatter.2
  196.2 61.2 reduce-scatter.4
where the time goes:
time: 340 us; the launch traced here: 339 us
  blocking collectives  285 us (84%)
  matrix products  22.1 us (6%)
  between operations  15.2 us (4%)
  other arithmetic  14.8 us (4%)
    psum x1, blocking collectives, body(): grad_cache = lax.psum(grad_latent, 'head').astype(jnp.bfloat16)  164 us
    all_gather x1, blocking collectives, body(): lax.all_gather(cotangent, 'ctx', axis=0, tiled=True)  32.5 us
    all_gather x1, blocking collectives, body(): lax.all_gather(rotated, 'ctx', axis=0, tiled=True)  30.6 us
    pmax x1, blocking collectives, body(): peak = lax.pmax(local_peak, 'ctx')  21.4 us
    psum x1, blocking collectives, body(): delta = lax.psum(local_delta, 'ctx')  19.1 us
    psum x1, blocking collectives, body(): mass = lax.psum(local_mass, 'ctx')  17.1 us
  transfers between devices with their start and end apart: 2, of which 0 were waited for; matrix products, arithmetic and copies ran while one was open for 4% of the time, Pallas kernels for 0%

commit v1 on v0

--- a/solution.py
+++ b/solution.py
@@ -81,7 +81,7 @@
     )
     grad_value = jnp.einsum("thk,thv->kv", prob_low, gradients, preferred_element_type=jnp.float32)
     grad_latent = grad_latent + jnp.pad(grad_value, ((0, 0), (0, extra_width)))
-    grad_cache = lax.psum(grad_latent, "head").astype(jnp.bfloat16)
+    grad_cache = jnp.sum(lax.all_gather(grad_latent, "head"), axis=0).astype(jnp.bfloat16)
     grad_rotated = lax.psum_scatter(grad_rotated, "ctx", scatter_dimension=0, tiled=True)
     grad_query = rotate(grad_rotated, cosines, sine_part, value_width, True)
     return (attention, grad_query, grad_cache)

time: 340 us -> 471 us (1.39)
  waiting for transfers between devices: 0.04 us -> 221 us
  blocking collectives: 285 us -> 121 us
  local copies, waits for them, and re-layouts: 2.48 us -> 46.8 us
  other arithmetic: 14.8 us -> 42.3 us
    psum x1 -> x0, blocking collectives: 164 us -> none  [body(): grad_cache = lax.psum(grad_latent, 'head').astype(jnp.bfloat16)]
    all_gather x0 -> x1, waiting for transfers between devices: none -> 129 us  [body(): lax.all_gather(grad_latent, 'head')]
    reduce_scatter x1, waiting for transfers between devices: 0.01 us -> 63.7 us  [body(): lax.psum_scatter(grad_rotated, 'ctx', scatter_dimension=0, tiled=True)]
    all_gather x0 -> x1, local copies, waits for them, and re-layouts: none -> 44.4 us  [body(): lax.all_gather(grad_latent, 'head')]
    reduce_scatter x1, waiting for transfers between devices: 0.01 us -> 27.8 us  [body(): lax.psum_scatter(attended, 'ctx', scatter_dimension=0, tiled=True)]
    reduce_sum x0 -> x1, other arithmetic: none -> 27.5 us  [body(): jnp.sum(lax.all_gather(grad_latent, 'head'), axis=0).astype(jnp.bfloat16)]
  transfers between devices with their start and end apart: 2 -> 3, of which waited for: 0 -> 3; matrix products, arithmetic and copies ran while one was open for 4% -> 4% of each run, Pallas kernels for 0% -> 0%
where the time goes in v1:
time: 471 us; the launch traced here: 470 us
  waiting for transfers between devices  221 us (47%)
  blocking collectives  121 us (26%)
  local copies, waits for them, and re-layouts  46.8 us (10%)
  other arithmetic  42.3 us (9%)
  matrix products  22 us (5%)
  between operations  16.7 us (4%)
    all_gather x1, waiting for transfers between devices, body(): lax.all_gather(grad_latent, 'head')  129 us
    reduce_scatter x1, waiting for transfers between devices, body(): lax.psum_scatter(grad_rotated, 'ctx', scatter_dimension=0, tiled=True)  63.7 us
    all_gather x1, local copies, waits for them, and re-layouts, body(): lax.all_gather(grad_latent, 'head')  44.4 us
    all_gather x1, blocking collectives, body(): lax.all_gather(cotangent, 'ctx', axis=0, tiled=True)  32.5 us
    all_gather x1, blocking collectives, body(): lax.all_gather(rotated, 'ctx', axis=0, tiled=True)  30.6 us
    reduce_scatter x1, waiting for transfers between devices, body(): lax.psum_scatter(attended, 'ctx', scatter_dimension=0, tiled=True)  27.8 us
    reduce_sum x1, other arithmetic, body(): jnp.sum(lax.all_gather(grad_latent, 'head'), axis=0).astype(jnp.bfloat16)  27.5 us
    pmax x1, blocking collectives, body(): peak = lax.pmax(local_peak, 'ctx')  21.4 us
  transfers between devices with their start and end apart: 3, of which 3 were waited for; matrix products, arithmetic and copies ran while one was open for 4% of the time, Pallas kernels for 0%

profile of v1, /device:TPU:0, one launch (start us, length us, event | category | flops | bytes accessed | tf_op | source)
XLA Modules:
  0.0 469.7 jit_solution(1641697301060233314)
XLA Ops:
  8.0 0.0 reduce-scatter.3.cloned.1.call-start
  9.2 0.7 slice.130
  9.9 0.7 convert_element_type.83
  10.6 32.5 %all_gather.13 = bf16[8,16,512]{2,1,0:T(8,128)(2,1)S(1)} all-gather(bf16[1,16,512]{2,1,0:T(8,128)(2,1)} %param.9), channel_id=1, replica_groups=mesh['ctx'=8,'head'=4] {'ctx'}, dimensions={0}, use_global_device_ids=true | all-gather | bytes 147456 | tf_op jit(solution)/shard_map/all_gather | solution.py:51
  43.2 0.7 fusion.15
  43.9 0.7 fusion.18
  44.6 0.7 fusion.22
  45.3 0.7 fusion.26
  46.1 0.7 fusion.30
  46.8 0.7 fusion.34
  47.6 0.7 fusion.38
  48.3 0.7 fusion.42
  49.1 0.7 fusion.50
  49.8 0.7 fusion.49
  50.5 0.1 subtract_convert_fusion
  50.6 0.1 pad_maximum_fusion.1
  50.7 30.6 %all_gather.12 = bf16[8,16,576]{2,1,0:T(8,128)(2,1)S(1)} all-gather(bf16[1,16,576]{2,1,0:T(8,128)(2,1)S(1)} %pad_maximum_fusion.1), channel_id=1, replica_groups=mesh['ctx'=8,'head'=4] {'ctx'}, dimensions={0}, use_global_device_ids=true | all-gather | bytes 165888 | tf_op jit(solution)/shard_map/all_gather | solution.py:50
  81.2 0.7 broadcast_compare_fusion
  82.0 3.6 fusion.69
  85.6 21.4 %pmax.7 = f32[8,16]{1,0:T(8,128)S(1)} all-reduce(f32[8,16]{1,0:T(8,128)S(1)} %get-tuple-element.36), channel_id=1, replica_groups=mesh['ctx'=8,'head'=4] {'ctx'}, use_global_device_ids=true, to_apply=%region_1.2 | all-reduce | flops 128 | bytes 1024 | tf_op jit(solution)/shard_map/pmax | solution.py:63
  107.0 0.0 slice-start
  107.0 0.6 fusion.11
  107.5 17.1 %psum.14 = f32[8,16]{1,0:T(8,128)S(1)} all-reduce(f32[8,16]{1,0:T(8,128)S(1)} %fusion.11), channel_id=1, replica_groups=mesh['ctx'=8,'head'=4] {'ctx'}, use_global_device_ids=true, to_apply=%region_3.4 | all-reduce | flops 128 | bytes 1024 | tf_op jit(solution)/shard_map/psum | solution.py:66
  124.7 0.0 slice-start.1
  124.7 4.9 %multiply_reduce_fusion = (f32[8,16]{1,0:T(8,128)S(1)}, bf16[8,16,4096]{2,1,0:T(8,128)(2,1)S(1)}, f32[8,16,4096]{2,1,0:T(8,128)}) fusion(f32[8,16]{1,0:T(8,128)S(1)} %psum.14, f32[8,16,4096]{2,1,0:T(8,128)S(1)} %get-tuple-element.37, f32[8,16]{1,0:T(8,128)S(1)} %pmax.7, pred[8,4096]{1,0:T(8,128)(4,1)S(1)} %broadcast_compare_fusion, ...), kind=kOutput, calls=%fused_computation.14 | convolution fusion | flops 540540800 | bytes 9602560 | tf_op jit(solution)/shard_map/thv,kv->thk/dot_general | solution.py:74
  129.5 0.0 copy-start
  129.5 1.0 copy-done
  130.5 0.0 slice-done
  130.5 0.0 slice-done.1
  130.5 2.3 fusion.6
  132.8 0.0 reduce-scatter.3.cloned.1.call-update
  132.8 0.0 reduce-scatter.5.cloned.1.call-start
  132.9 19.1 %psum.15 = f32[8,16]{1,0:T(8,128)S(1)} all-reduce(f32[8,16]{1,0:T(8,128)S(1)} %get-tuple-element.7), channel_id=1, replica_groups=mesh['ctx'=8,'head'=4] {'ctx'}, use_global_device_ids=true, to_apply=%region_6.7 | all-reduce | flops 128 | bytes 1024 | tf_op jit(solution)/shard_map/psum | solution.py:76
  152.0 2.3 multiply_convert_fusion
  154.4 0.0 copy-start.1
  154.4 4.9 %fusion.1 = f32[8,16,576]{2,1,0:T(8,128)} fusion(bf16[8,16,4096]{2,1,0:T(8,128)(2,1)S(1)} %multiply_convert_fusion, bf16[4096,576]{0,1:T(8,128)(2,1)} %param.8), kind=kOutput, calls=%fused_computation.4 | convolution fusion | flops 603979776 | bytes 6062080 | tf_op jit(solution)/shard_map/thk,kl->thl/dot_general | solution.py:78
  159.3 0.0 reduce-scatter.5.cloned.1.call-update
  159.3 0.2 all-gather.3.cloned.1.call-start
  159.6 0.0 copy-done.1
  159.6 1.3 convolution_bitcast_fusion
  160.9 5.1 %bitcast_add_fusion = f32[4096,576]{0,1:T(8,128)} fusion(f32[4096,512]{0,1:T(8,128)S(1)} %convolution_bitcast_fusion, bf16[8,16,4096]{2,1,0:T(8,128)(2,1)S(1)} %multiply_convert_fusion, bf16[8,16,576]{2,1,0:T(8,128)(2,1)S(1)} %all_gather.12), kind=kOutput, calls=%fused_computation | convolution fusion | flops 606339072 | bytes 19021824 | tf_op jit(solution)/shard_map/thk,thl->kl/dot_general | solution.py:79
  165.9 0.0 all-gather.3.cloned.1.call-update
  165.9 27.8 %reduce-scatter.3.cloned.1.call-done = f32[1,16,512]{2,1,0:T(8,128)} async-done(((f32[8,16,512]{2,1,0:T(8,128)}), f32[1,16,512]{2,1,0:T(8,128)}) %reduce-scatter.3.cloned.1.call-update) | async-done | bytes 32784 | tf_op jit(solution)/shard_map/reduce_scatter | solution.py:71
  193.8 1.4 convert_element_type.103
  195.1 63.7 %reduce-scatter.5.cloned.1.call-done = f32[1,16,576]{2,1,0:T(8,128)} async-done(((f32[8,16,576]{2,1,0:T(8,128)}), f32[1,16,576]{2,1,0:T(8,128)}) %reduce-scatter.5.cloned.1.call-update) | async-done | bytes 36880 | tf_op jit(solution)/shard_map/reduce_scatter | solution.py:85
  258.8 0.8 slice.175
  259.6 0.8 multiply_subtract_fusion
  260.4 0.7 pad_maximum_fusion
  261.1 129.3 %all-gather.3.cloned.1.call-done = f32[16384,576]{0,1:T(8,128)} async-done(((f32[4096,576]{0,1:T(8,128)}), f32[16384,576]{0,1:T(8,128)}) %all-gather.3.cloned.1.call-update) | async-done | bytes 37748752 | tf_op jit(solution)/shard_map/all_gather | solution.py:84
  390.4 44.4 %reshape.294 = f32[4,4096,576]{1,0,2:T(4,128)} reshape(f32[16384,576]{0,1:T(8,128)} %all-gather.3.cloned.1.call-done) | data formatting | bytes 75497472 | tf_op jit(solution)/shard_map/all_gather | solution.py:84
  434.8 27.5 %reduce_sum.29 = bf16[4096,576]{0,1:T(8,128)(2,1)} reduce(f32[4,4096,576]{1,0,2:T(4,128)} %reshape.294, f32[]{:T(128)} %constant.447.clone.1), dimensions={0}, to_apply=%region_8.9 | reduce | flops 7077888 | bytes 42467332 | tf_op jit(solution)/shard_map/reduce_sum | solution.py:84
  (2 shorter events, 0.0 us)
Async XLA Ops:
  8.0 185.8 %reduce-scatter.3.cloned.1.call-start = ((), (), s32[]{:S(2)}) async-start(), calls=%async_computation.2 | async-start | bytes 294912 | tf_op jit(solution)/shard_map/reduce_scatter | solution.py:71
  107.0 23.6 %slice-start = ((s8[4718592]{0:T(1024)(128)(4,1)}), s8[524288]{0:T(1024)(128)(4,1)S(1)}, s32[]{:S(2)}) async-start(s8[4718592]{0:T(1024)(128)(4,1)} %bitcast.53), calls=%async_computation.5 | async-start | bytes 1048576
  124.7 5.8 %slice-start.1 = ((s8[4718592]{0:T(1024)(128)(4,1)}), s8[4194304]{0:T(1024)(128)(4,1)S(1)}, s32[]{:S(2)}) async-start(s8[4718592]{0:T(1024)(128)(4,1)} %bitcast.53), calls=%async_computation.6 | async-start | bytes 8388608
  129.5 1.0 copy-start
  132.8 126.0 %reduce-scatter.5.cloned.1.call-start = ((), (), s32[]{:S(2)}) async-start(), calls=%async_computation.3 | async-start | bytes 368640 | tf_op jit(solution)/shard_map/reduce_scatter | solution.py:85
  154.4 5.2 %copy-start.1 = (bf16[8,16,4096]{2,1,0:T(8,128)(2,1)S(1)}, bf16[8,16,4096]{2,1,0:T(8,128)(2,1)}, u32[]{:S(2)}) copy-start(bf16[8,16,4096]{2,1,0:T(8,128)(2,1)} %copy-done) | copy-start | bytes 3145732
  159.3 231.1 %all-gather.3.cloned.1.call-start = ((), (), s32[]{:S(2)}) async-start(), calls=%async_computation.4 | async-start | bytes 47185920 | tf_op jit(solution)/shard_map/all_gather | solution.py:84
Sparse Core Ops, SparseCore 0:
  133.0 60.7 reduce-scatter.2
  197.6 61.1 reduce-scatter.4
Sparse Core Ops, SparseCore 1:
  166.0 224.3 all-gather.2
